TPU v7x, 512 devices: a whole 4x4x16 slice. The times are simulated.
512 devices in a mesh: seq: 64 (over z, y), tp: 8 (over x, core).
Axes of the slice: x: 4, y: 4, z: 16, core: 2. Of those that a mesh axis runs over, the one named last changes fastest.
Arguments:
- query_proj: bfloat16 [4096, 8192], P('tp', 'seq'), may hold values from -6 to 6
- key_proj: bfloat16 [4096, 8192], P('tp', 'seq'), may hold values from -6 to 6
- value_proj: bfloat16 [4096, 8192], P('tp', 'seq'), may hold values from -6 to 6
- short_taps: float32 [3, 3, 4096], P(None, None, 'tp'), may hold values from -3.5 to 3.5
- long_filters: float32 [4096, 8192], P(('tp', 'seq')), may hold values from -2 to 2
- out_weight: bfloat16 [4096, 8192], P('seq', 'tp'), may hold values from -0.09375 to 0.09375
Outputs:
- block_out: bfloat16 [8192, 8192], P('seq', 'tp')
All inputs are finite; a program needn't handle non-finite values.
Results may differ from a plain program's by a relative error of at most 0.0058.
Values may be sent and summed in bfloat16 or wider, within the bound.
A program may use at most 64 MiB of HBM per device.

v0:
```python
import math
import jax
import jax.numpy as jnp
from jax import lax
from jax.sharding import PartitionSpec as P

precise = lax.Precision.HIGHEST


def shifted(value, axis, steps):
    count = lax.axis_size(axis)
    initial, last = (max(0, -steps), min(count, count - steps))
    return lax.ppermute(value, axis, [(source, source + steps) for source in range(initial, last)])


def short_filter(extended, tap_weights):
    return (
        tap_weights[0][:, None] * extended[:, 2:]
        + tap_weights[1][:, None] * extended[:, 1:-1]
        + tap_weights[2][:, None] * extended[:, :-2]
    )


def phase_table(period, out_size, in_size, direction):
    out_index = lax.broadcasted_iota(jnp.int32, (out_size, in_size), 0)
    in_index = lax.broadcasted_iota(jnp.int32, (out_size, in_size), 1)
    phase_angle = (out_index * in_index % period).astype(jnp.float32) * (
        direction * 2.0 * math.pi / period
    )
    return (jnp.cos(phase_angle), jnp.sin(phase_angle))


def left_apply(phase, signal):
    return jnp.einsum("kn,cnm->ckm", phase, signal, precision=precise)


def right_apply(signal, phase):
    return jnp.einsum("ckn,nm->ckm", signal, phase, precision=precise)


def forward_spectrum(signal, inner_size):
    channels_here, length = signal.shape
    period = 2 * length
    outer_size = period // inner_size
    blocks = signal.reshape(channels_here, outer_size // 2, inner_size)
    left_re, left_im = phase_table(outer_size, outer_size, outer_size // 2, -1.0)
    section_re = left_apply(left_re, blocks)
    section_im = left_apply(left_im, blocks)
    twist_re, twist_im = phase_table(period, outer_size, inner_size, -1.0)
    turned_re = section_re * twist_re - section_im * twist_im
    turned_im = section_re * twist_im + section_im * twist_re
    right_re, right_im = phase_table(inner_size, inner_size, inner_size, -1.0)
    spec_re = right_apply(turned_re, right_re) - right_apply(turned_im, right_im)
    spec_im = right_apply(turned_re, right_im) + right_apply(turned_im, right_re)
    return (spec_re, spec_im)


def inverse_signal(spec_re, spec_im, length, inner_size):
    channels_here = spec_re.shape[0]
    period = 2 * length
    outer_size = period // inner_size
    right_re, right_im = phase_table(inner_size, inner_size, inner_size, 1.0)
    mid_re = right_apply(spec_re, right_re) - right_apply(spec_im, right_im)
    mid_im = right_apply(spec_re, right_im) + right_apply(spec_im, right_re)
    twist_re, twist_im = phase_table(period, outer_size, inner_size, 1.0)
    turned_re = mid_re * twist_re - mid_im * twist_im
    turned_im = mid_re * twist_im + mid_im * twist_re
    left_re, left_im = phase_table(outer_size, outer_size // 2, outer_size, 1.0)
    signal = left_apply(left_re, turned_re) - left_apply(left_im, turned_im)
    return signal.reshape(channels_here, length) / period


def long_convolve(signal, filters, inner_size):
    length = signal.shape[1]
    data_re, data_im = forward_spectrum(signal, inner_size)
    filt_re, filt_im = forward_spectrum(filters, inner_size)
    prod_re = data_re * filt_re - data_im * filt_im
    prod_im = data_re * filt_im + data_im * filt_re
    return inverse_signal(prod_re, prod_im, length, inner_size)


def shards(query_proj, key_proj, value_proj, short_taps, long_filters, out_weight):
    tok_rows = query_proj.shape[1]
    inner_size = tok_rows // 2
    tail_cols = jnp.stack([query_proj[:, -2:], key_proj[:, -2:], value_proj[:, -2:]])
    before = shifted(tail_cols, "seq", 1)
    shorts = []
    for stream_index, stream in enumerate((query_proj, key_proj, value_proj)):
        extended = jnp.concatenate([before[stream_index], stream], axis=1).astype(jnp.float32)
        shorts.append(short_filter(extended, short_taps[stream_index]))
    query_short, key_short, value_short = shorts
    product = (key_short * value_short).astype(jnp.bfloat16)
    spread = lax.all_to_all(product, "seq", split_axis=0, concat_axis=1, tiled=True)
    mixed_conv = long_convolve(spread.astype(jnp.float32), long_filters, inner_size)
    returned = lax.all_to_all(mixed_conv, "seq", split_axis=1, concat_axis=0, tiled=True)
    gated_out = (query_short * returned).astype(jnp.bfloat16)
    full_rows = lax.all_gather(gated_out, "tp", axis=0, tiled=True)
    result = lax.dot_general(
        full_rows,
        lax.all_gather(out_weight, "seq", axis=0, tiled=True),
        (((0,), (0,)), ((), ())),
        preferred_element_type=jnp.float32,
    )
    return result.astype(jnp.bfloat16)


def solution(mesh):
    return jax.shard_map(
        shards,
        mesh=mesh,
        in_specs=(
            P("tp", "seq"),
            P("tp", "seq"),
            P("tp", "seq"),
            P(None, None, "tp"),
            P(("tp", "seq"), None),
            P("seq", "tp"),
        ),
        out_specs=P("seq", "tp"),
        check_vma=False,
    )
```

profile of v0, /device:TPU:2, one launch (start us, length us, event | category | flops | bytes accessed | tf_op | source)
XLA Modules:
  0.0 292.9 jit_solution(1270531788461723805)
XLA Ops:
  6.5 1.0 slice.94
  7.7 1.0 slice.95
  8.8 1.0 slice.96
  10.3 3.5 %collective-permute-start = (bf16[3,512,2]{2,1,0:T(8,128)(2,1)S(1)}, bf16[3,512,2]{2,1,0:T(8,128)(2,1)S(1)}, u32[]{:S(2)}, u32[]{:S(2)}) collective-permute-start(bf16[3,512,2]{2,1,0:T(8,128)(2,1)S(1)} %copy.25), channel_id=1, source_target_pairs={{0,8},{8,16},{16,24},{24,32},{32,40},{40,48},{48,56},{56,64},{64,7... | collective-permute-start | bytes 18440 | tf_op jit(solution)/shard_map/ppermute | solution.py:13
  14.1 1.1 reshape.82
  15.4 1.1 fusion.58
  16.5 1.1 fusion.61
  17.6 0.9 fusion.180
  20.3 1.8 collective-permute-done
  22.4 1.4 fusion.47
  23.8 20.5 %all-to-all-start = ((bf16[64,8,128]{2,1,0:T(8,128)(2,1)}), bf16[64,8,128]{2,1,0:T(8,128)(2,1)S(1)}, u32[]{:S(2)}, u32[]{:S(2)}) async-start(bf16[64,8,128]{2,1,0:T(8,128)(2,1)} %fusion.47), calls=%async_computation | async-start | bytes 262144 | tf_op jit(solution)/shard_map/all_to_all | solution.py:93
  45.9 15.1 %all-to-all-done = bf16[64,8,128]{2,1,0:T(8,128)(2,1)S(1)} async-done(((bf16[64,8,128]{2,1,0:T(8,128)(2,1)}), bf16[64,8,128]{2,1,0:T(8,128)(2,1)S(1)}, u32[]{:S(2)}, u32[]{:S(2)}) %all-to-all-start) | async-done | bytes 131104 | tf_op jit(solution)/shard_map/all_to_all | solution.py:93
  61.1 0.9 convolution_bitcast_fusion
  62.0 0.9 convolution_bitcast_fusion.1
  65.3 0.9 multiply_add_fusion
  69.2 1.1 fusion.11
  70.3 1.1 fusion.1
  71.7 1.1 copy.32
  72.8 4.6 %all-to-all-start.1 = ((f32[8,64,128]{2,0,1:T(8,128)}), f32[8,64,128]{2,0,1:T(8,128)S(1)}, u32[]{:S(2)}, u32[]{:S(2)}) async-start(f32[8,64,128]{2,0,1:T(8,128)} %copy.32), calls=%async_computation.1 | async-start | bytes 524288 | tf_op jit(solution)/shard_map/all_to_all | solution.py:95
  77.6 21.1 %all-to-all-done.1 = f32[8,64,128]{2,0,1:T(8,128)S(1)} async-done(((f32[8,64,128]{2,0,1:T(8,128)}), f32[8,64,128]{2,0,1:T(8,128)S(1)}, u32[]{:S(2)}, u32[]{:S(2)}) %all-to-all-start.1) | async-done | bytes 262176 | tf_op jit(solution)/shard_map/all_to_all | solution.py:95
  98.8 1.1 fusion.23
  100.6 19.3 %all-gather.3.cloned.1.call-done = bf16[4096,128]{1,0:T(8,128)(2,1)} async-done(((bf16[512,128]{1,0:T(8,128)(2,1)}), bf16[4096,128]{1,0:T(8,128)(2,1)}) %all-gather.3.cloned.1.call-update) | async-done | bytes 1048592 | tf_op jit(solution)/shard_map/all_gather | solution.py:97
  120.0 160.3 %all-gather.5.cloned.1.call-done = bf16[4096,1024]{1,0:T(8,128)(2,1)} async-done(((bf16[64,1024]{1,0:T(8,128)(2,1)}), bf16[4096,1024]{1,0:T(8,128)(2,1)}) %all-gather.5.cloned.1.call-update) | async-done | bytes 8388624 | tf_op jit(solution)/shard_map/all_gather | solution.py:100
  280.3 5.7 %convolution_convert_fusion = bf16[128,1024]{1,0:T(8,128)(2,1)} fusion(bf16[4096,128]{1,0:T(8,128)(2,1)} %all-gather.3.cloned.1.call-done, bf16[4096,1024]{1,0:T(8,128)(2,1)} %all-gather.5.cloned.1.call-done), kind=kOutput, calls=%fused_computation.8 | convolution fusion | flops 1073872896 | bytes 9699328 | tf_op jit(solution)/shard_map/dot_general | solution.py:98
  (36 shorter events, 11.4 us)
Async XLA Ops:
  6.5 15.6 %copy-start.1 = (bf16[512,128]{1,0:T(8,128)(2,1)S(1)}, bf16[512,128]{1,0:T(8,128)(2,1)}, u32[]{:S(2)}) copy-start(bf16[512,128]{1,0:T(8,128)(2,1)} %param.7) | copy-start | bytes 393220
  6.5 15.6 %copy-start = (bf16[512,128]{1,0:T(8,128)(2,1)S(1)}, bf16[512,128]{1,0:T(8,128)(2,1)}, u32[]{:S(2)}) copy-start(bf16[512,128]{1,0:T(8,128)(2,1)} %param.8) | copy-start | bytes 393220
  10.3 11.8 %collective-permute-start = (bf16[3,512,2]{2,1,0:T(8,128)(2,1)S(1)}, bf16[3,512,2]{2,1,0:T(8,128)(2,1)S(1)}, u32[]{:S(2)}, u32[]{:S(2)}) collective-permute-start(bf16[3,512,2]{2,1,0:T(8,128)(2,1)S(1)} %copy.25), channel_id=1, source_target_pairs={{0,8},{8,16},{16,24},{24,32},{32,40},{40,48},{48,56},{56,64},{64,7... | collective-permute-start | bytes 18440 | tf_op jit(solution)/shard_map/ppermute | solution.py:13
  23.8 37.2 %all-to-all-start = ((bf16[64,8,128]{2,1,0:T(8,128)(2,1)}), bf16[64,8,128]{2,1,0:T(8,128)(2,1)S(1)}, u32[]{:S(2)}, u32[]{:S(2)}) async-start(bf16[64,8,128]{2,1,0:T(8,128)(2,1)} %fusion.47), calls=%async_computation | async-start | bytes 262144 | tf_op jit(solution)/shard_map/all_to_all | solution.py:93
  64.5 13.0 %copy-start.2 = (bf16[512,128]{1,0:T(8,128)(2,1)S(1)}, bf16[512,128]{1,0:T(8,128)(2,1)}, u32[]{:S(2)}) copy-start(bf16[512,128]{1,0:T(8,128)(2,1)} %param.6) | copy-start | bytes 393220
  72.8 26.0 %all-to-all-start.1 = ((f32[8,64,128]{2,0,1:T(8,128)}), f32[8,64,128]{2,0,1:T(8,128)S(1)}, u32[]{:S(2)}, u32[]{:S(2)}) async-start(f32[8,64,128]{2,0,1:T(8,128)} %copy.32), calls=%async_computation.1 | async-start | bytes 524288 | tf_op jit(solution)/shard_map/all_to_all | solution.py:95
  77.4 42.5 %all-gather.3.cloned.1.call-start = ((), (), s32[]{:S(2)}) async-start(), calls=%async_computation.2 | async-start | bytes 1179648 | tf_op jit(solution)/shard_map/all_gather | solution.py:97
  99.9 180.4 %all-gather.5.cloned.1.call-start = ((), (), s32[]{:S(2)}) async-start(), calls=%async_computation.3 | async-start | bytes 8519680 | tf_op jit(solution)/shard_map/all_gather | solution.py:100
Sparse Core Ops, SparseCore 0:
  100.0 19.9 all-gather.2
  122.9 157.3 all-gather.4
where the time goes:
time: 293 us
  waiting for transfers between devices  218 us (74%)
  starting transfers between devices  28.7 us (10%)
  matrix products  21.1 us (7%)
  between operations  13.7 us (5%)
  local copies, waits for them, and re-layouts  7.47 us (3%)
  other arithmetic  3.41 us (1%)
    all_gather x1, waiting for transfers between devices, shards(): lax.all_gather(out_weight, 'seq', axis=0, tiled=True)  160 us
    all_to_all x1, waiting for transfers between devices, shards(): lax.all_to_all(mixed_conv, 'seq', split_axis=1, concat_axis=0, tiled=True)  21.1 us
    all_to_all x1, starting transfers between devices, shards(): lax.all_to_all(product, 'seq', split_axis=0, concat_axis=1, tiled=True)  20.5 us
    all_gather x1, waiting for transfers between devices, shards(): full_rows = lax.all_gather(gated_out, 'tp', axis=0, tiled=True)  19.3 us
    all_to_all x1, waiting for transfers between devices, shards(): lax.all_to_all(product, 'seq', split_axis=0, concat_axis=1, tiled=True)  15.1 us
    dot_general x12, matrix products, right_apply(): return jnp.einsum('ckn,nm->ckm', signal, phase, precision=precise)  9.29 us
  transfers between devices with their start and end apart: 5, of which 5 were waited for; matrix products, arithmetic and copies ran while one was open for 3% of the time, Pallas kernels for 0%

commit v1 on v0

--- a/solution.py
+++ b/solution.py
@@ -1,3 +1,4 @@
+import functools
 import math
 import jax
 import jax.numpy as jnp
@@ -5,6 +6,15 @@
 from jax.sharding import PartitionSpec as P
 
 precise = lax.Precision.HIGHEST
+
+
+def make_corner(panel, comm_axis):
+    return jnp.concatenate(
+        jax.lax.all_to_all(jnp.stack([panel] * jax.lax.axis_size(comm_axis), 0), comm_axis, 0, 0), 0
+    )
+
+
+post_the_cubes = functools.partial(make_corner, comm_axis="tp")
 
 
 def shifted(value, axis, steps):
@@ -94,7 +104,7 @@
     mixed_conv = long_convolve(spread.astype(jnp.float32), long_filters, inner_size)
     returned = lax.all_to_all(mixed_conv, "seq", split_axis=1, concat_axis=0, tiled=True)
     gated_out = (query_short * returned).astype(jnp.bfloat16)
-    full_rows = lax.all_gather(gated_out, "tp", axis=0, tiled=True)
+    full_rows = post_the_cubes(gated_out)
     result = lax.dot_general(
         full_rows,
         lax.all_gather(out_weight, "seq", axis=0, tiled=True),

time: 293 us -> 186 us (0.63)
  waiting for transfers between devices: 218 us -> 92.7 us
  blocking collectives: 0 us -> 19.5 us
    all_gather x1, waiting for transfers between devices: 160 us -> 52.6 us  [shards(): lax.all_gather(out_weight, 'seq', axis=0, tiled=True)]
    all_to_all x0 -> x1, blocking collectives: none -> 19.5 us  [make_corner(): jax.lax.all_to_all(jnp.stack([panel] * jax.lax.axis_size(comm_axis), 0),...]
    all_gather x1 -> x0, waiting for transfers between devices: 19.3 us -> none  [shards(): full_rows = lax.all_gather(gated_out, 'tp', axis=0, tiled=True)]
  transfers between devices with their start and end apart: 5 -> 4, of which waited for: 5 -> 4; matrix products, arithmetic and copies ran while one was open for 3% -> 14% of each run, Pallas kernels for 0% -> 0%
where the time goes in v1:
time: 186 us
  waiting for transfers between devices  92.7 us (50%)
  starting transfers between devices  28.7 us (15%)
  matrix products  20.8 us (11%)
  blocking collectives  19.5 us (10%)
  between operations  13.7 us (7%)
  local copies, waits for them, and re-layouts  7.57 us (4%)
  other arithmetic  2.75 us (1%)
    all_gather x1, waiting for transfers between devices, shards(): lax.all_gather(out_weight, 'seq', axis=0, tiled=True)  52.6 us
    all_to_all x1, waiting for transfers between devices, shards(): lax.all_to_all(mixed_conv, 'seq', split_axis=1, concat_axis=0, tiled=True)  21.7 us
    all_to_all x1, starting transfers between devices, shards(): lax.all_to_all(product, 'seq', split_axis=0, concat_axis=1, tiled=True)  20.5 us
    all_to_all x1, blocking collectives, make_corner(): jax.lax.all_to_all(jnp.stack([panel] * jax.lax.axis_size(comm_axis), 0),...  19.5 us
    all_to_all x1, waiting for transfers between devices, shards(): lax.all_to_all(product, 'seq', split_axis=0, concat_axis=1, tiled=True)  16 us
    dot_general x12, matrix products, right_apply(): return jnp.einsum('ckn,nm->ckm', signal, phase, precision=precise)  9.3 us
    dot_general x1, matrix products, shards(): lax.dot_general(full_rows, lax.all_gather(out_weight, 'seq', axis=0, tile...  5.36 us
    all_to_all x1, starting transfers between devices, shards(): lax.all_to_all(mixed_conv, 'seq', split_axis=1, concat_axis=0, tiled=True)  4.7 us
  transfers between devices with their start and end apart: 4, of which 4 were waited for; matrix products, arithmetic and copies ran while one was open for 14% of the time, Pallas kernels for 0%

profile of v1, /device:TPU:2, one launch (start us, length us, event | category | flops | bytes accessed | tf_op | source)
XLA Modules:
  0.0 185.7 jit_solution(9408293760398823729)
XLA Ops:
  7.3 1.0 slice.94
  8.4 1.0 slice.95
  9.5 1.0 slice.96
  10.9 3.5 %collective-permute-start = (bf16[3,512,2]{2,1,0:T(8,128)(2,1)S(1)}, bf16[3,512,2]{2,1,0:T(8,128)(2,1)S(1)}, u32[]{:S(2)}, u32[]{:S(2)}) collective-permute-start(bf16[3,512,2]{2,1,0:T(8,128)(2,1)S(1)} %copy.25), channel_id=1, source_target_pairs={{0,8},{8,16},{16,24},{24,32},{32,40},{40,48},{48,56},{56,64},{64,7... | collective-permute-start | bytes 18440 | tf_op jit(solution)/shard_map/ppermute | solution.py:23
  14.5 1.1 reshape.87
  16.1 0.9 fusion.180
  17.0 1.1 fusion.58
  18.0 1.1 fusion.61
  21.0 1.8 collective-permute-done
  23.1 1.4 fusion.47
  24.5 20.5 %all-to-all-start = ((bf16[64,8,128]{2,1,0:T(8,128)(2,1)}), bf16[64,8,128]{2,1,0:T(8,128)(2,1)S(1)}, u32[]{:S(2)}, u32[]{:S(2)}) async-start(bf16[64,8,128]{2,1,0:T(8,128)(2,1)} %fusion.47), calls=%async_computation | async-start | bytes 262144 | tf_op jit(solution)/shard_map/all_to_all | solution.py:103
  45.0 0.8 fusion.6
  46.6 16.0 %all-to-all-done = bf16[64,8,128]{2,1,0:T(8,128)(2,1)S(1)} async-done(((bf16[64,8,128]{2,1,0:T(8,128)(2,1)}), bf16[64,8,128]{2,1,0:T(8,128)(2,1)S(1)}, u32[]{:S(2)}, u32[]{:S(2)}) %all-to-all-start) | async-done | bytes 131104 | tf_op jit(solution)/shard_map/all_to_all | solution.py:103
  62.7 0.9 convolution_bitcast_fusion
  63.6 0.9 convolution_bitcast_fusion.1
  66.9 0.9 multiply_add_fusion
  70.8 1.1 fusion.11
  71.9 1.1 fusion.1
  73.3 1.1 copy.32
  74.4 4.7 %all-to-all-start.1 = ((f32[8,64,128]{2,0,1:T(8,128)}), f32[8,64,128]{2,0,1:T(8,128)S(1)}, u32[]{:S(2)}, u32[]{:S(2)}) async-start(f32[8,64,128]{2,0,1:T(8,128)} %copy.32), calls=%async_computation.1 | async-start | bytes 524288 | tf_op jit(solution)/shard_map/all_to_all | solution.py:105
  79.3 21.7 %all-to-all-done.1 = f32[8,64,128]{2,0,1:T(8,128)S(1)} async-done(((f32[8,64,128]{2,0,1:T(8,128)}), f32[8,64,128]{2,0,1:T(8,128)S(1)}, u32[]{:S(2)}, u32[]{:S(2)}) %all-to-all-start.1) | async-done | bytes 262176 | tf_op jit(solution)/shard_map/all_to_all | solution.py:105
  101.5 19.5 %all_to_all.37 = bf16[8,512,128]{2,1,0:T(8,128)(2,1)S(1)} all-to-all(bf16[8,512,128]{2,1,0:T(8,128)(2,1)S(1)} %stack.27), channel_id=1, replica_groups=mesh['seq'=64,'tp'=8] {'tp'}, dimensions={0} | all-to-all | bytes 2097152 | tf_op jit(solution)/shard_map/all_to_all | solution.py:13
  121.0 52.6 %all-gather.2.cloned.1.call-done = bf16[4096,1024]{1,0:T(8,128)(2,1)} async-done(((bf16[64,1024]{1,0:T(8,128)(2,1)}), bf16[4096,1024]{1,0:T(8,128)(2,1)}) %all-gather.2.cloned.1.call-update) | async-done | bytes 8388624 | tf_op jit(solution)/shard_map/all_gather | solution.py:110
  173.5 5.4 %convolution_convert_fusion = bf16[128,1024]{1,0:T(8,128)(2,1)} fusion(bf16[4096,128]{1,0:T(8,128)(2,1)S(1)} %bitcast.109, bf16[4096,1024]{1,0:T(8,128)(2,1)} %all-gather.2.cloned.1.call-done), kind=kOutput, calls=%fused_computation.8 | convolution fusion | flops 1073872896 | bytes 9699328 | tf_op jit(solution)/shard_map/dot_general | solution.py:108
  (35 shorter events, 11.1 us)
Async XLA Ops:
  6.5 16.3 %copy-start.1 = (bf16[512,128]{1,0:T(8,128)(2,1)S(1)}, bf16[512,128]{1,0:T(8,128)(2,1)}, u32[]{:S(2)}) copy-start(bf16[512,128]{1,0:T(8,128)(2,1)} %param.7) | copy-start | bytes 393220
  6.5 16.3 %copy-start = (bf16[512,128]{1,0:T(8,128)(2,1)S(1)}, bf16[512,128]{1,0:T(8,128)(2,1)}, u32[]{:S(2)}) copy-start(bf16[512,128]{1,0:T(8,128)(2,1)} %param.8) | copy-start | bytes 393220
  6.5 167.0 %all-gather.2.cloned.1.call-start = ((), (), s32[]{:S(2)}) async-start(), calls=%async_computation.3 | async-start | bytes 8519680 | tf_op jit(solution)/shard_map/all_gather | solution.py:110
  10.9 11.8 %collective-permute-start = (bf16[3,512,2]{2,1,0:T(8,128)(2,1)S(1)}, bf16[3,512,2]{2,1,0:T(8,128)(2,1)S(1)}, u32[]{:S(2)}, u32[]{:S(2)}) collective-permute-start(bf16[3,512,2]{2,1,0:T(8,128)(2,1)S(1)} %copy.25), channel_id=1, source_target_pairs={{0,8},{8,16},{16,24},{24,32},{32,40},{40,48},{48,56},{56,64},{64,7... | collective-permute-start | bytes 18440 | tf_op jit(solution)/shard_map/ppermute | solution.py:23
  24.5 38.1 %all-to-all-start = ((bf16[64,8,128]{2,1,0:T(8,128)(2,1)}), bf16[64,8,128]{2,1,0:T(8,128)(2,1)S(1)}, u32[]{:S(2)}, u32[]{:S(2)}) async-start(bf16[64,8,128]{2,1,0:T(8,128)(2,1)} %fusion.47), calls=%async_computation | async-start | bytes 262144 | tf_op jit(solution)/shard_map/all_to_all | solution.py:103
  66.1 13.0 %copy-start.2 = (bf16[512,128]{1,0:T(8,128)(2,1)S(1)}, bf16[512,128]{1,0:T(8,128)(2,1)}, u32[]{:S(2)}) copy-start(bf16[512,128]{1,0:T(8,128)(2,1)} %param.6) | copy-start | bytes 393220
  74.4 26.5 %all-to-all-start.1 = ((f32[8,64,128]{2,0,1:T(8,128)}), f32[8,64,128]{2,0,1:T(8,128)S(1)}, u32[]{:S(2)}, u32[]{:S(2)}) async-start(f32[8,64,128]{2,0,1:T(8,128)} %copy.32), calls=%async_computation.1 | async-start | bytes 524288 | tf_op jit(solution)/shard_map/all_to_all | solution.py:105
Sparse Core Ops, SparseCore 0:
  10.3 163.2 all-gather.1
